TPU v7x, 32 devices: a whole 2x2x4 slice. The times are simulated.
32 devices in a mesh: groups: 2 (over y), span: 4 (over z), head: 2 (over x), slab: 2 (over core).
Axes of the slice: x: 2, y: 2, z: 4, core: 2. Of those that a mesh axis runs over, the one named last changes fastest.
Arguments:
- queries: bfloat16 [3072, 5120], P(('groups', 'span'), 'head'), parts along dimension 0, may hold values from -6 to 6
- keys: bfloat16 [3072, 5120], P(('groups', 'span', 'slab'), 'head'), parts along dimension 0, may hold values from -4 to 4
- values: bfloat16 [3072, 5120], P(('groups', 'span', 'slab'), 'head'), parts along dimension 0, may hold values from -240 to 240
- span_mask: int32 [8, 4], P('groups'), parts along dimension 0, may hold values from 0 to 1, as said below
- head_gain: float32 [5120], P('head'), may hold values from 0.5 to 2
- head_shift: float32 [5120], P('head'), may hold values from -3 to 3
- patch_weight: bfloat16 [5120, 64], P('head'), may hold values from -0.078125 to 0.078125
- noisy_latent: float32 [24, 16, 32, 16], P(('groups', 'span'), 'head', 'slab'), parts along dimension 0, may hold values from -6 to 6
- conv_weight: bfloat16 [432, 384], replicated, may hold values from -0.3125 to 0.3125
- conv_bias: float32 [384], replicated, may hold values from -3 to 3
Outputs:
- clean_latent: float32 [24, 16, 32, 16], P(('groups', 'span'), 'head', 'slab'), parts along dimension 0
- decoded: bfloat16 [24, 16, 32, 384], P(('groups', 'span'), 'head', 'slab'), parts along dimension 0
There are 2 independent parts, one for each index of `groups`. A program takes and returns all parts, laid end to end along the dimension named above; an argument that names none is the same for every part. Nothing has to cross between parts.
Inputs may be any that keep to these rules, and one draw needn't show every extreme that they name: span_mask[i, j] is 1 where j = i and 0 where j > i.
All inputs are finite; a program needn't handle non-finite values.
Results may differ from a plain program's by a relative error of at most 0.012.
Values may be sent and summed in bfloat16 or wider, within the bound.
No kernel may reach another device: no remote copies, remote signals or barrier semaphores. Data moves between devices by JAX's collectives and lax.ppermute only.
A program may use at most 128 MiB of HBM per device.

v0:
```python
import math
import jax
import jax.numpy as jnp
from jax import lax
from jax.sharding import PartitionSpec as P

HEADS = 40
HD = 128
LAT_CH = 16
FRAMES_SPAN = 3
TROWS = 8
TCOLS = 16
neg_big = -1e30
noise_level = 0.75
norm_eps = 1e-06


def with_halo(cells, sides, width):
    for axis, dim in sides:
        count = lax.axis_size(axis)
        ends = count - 1
        head = lax.slice_in_dim(cells, 0, width, axis=dim)
        tail = lax.slice_in_dim(cells, cells.shape[dim] - width, cells.shape[dim], axis=dim)
        cells = jnp.concatenate(
            [
                lax.ppermute(tail, axis, [(i, (i + 1) % count) for i in range(ends)]),
                cells,
                lax.ppermute(head, axis, [((i + 1) % count, i) for i in range(ends)]),
            ],
            axis=dim,
        )
    return cells


def from_behind(value, axis, by):
    size = lax.axis_size(axis)
    pairs = [(i, i + by) for i in range(size) if 0 <= i + by < size]
    return lax.ppermute(value, axis, pairs)


def block_length(total_rows):
    block_size = total_rows
    while block_size > 768 and block_size % 2 == 0:
        block_size = block_size // 2
    return block_size


def fold_keys(partial_state, key_value, query_block, mask_row, rows_span):
    keys_piece, values_piece = key_value
    heads_dev = query_block.shape[1]
    piece_rows = keys_piece.shape[0]
    length = block_length(piece_rows)
    span_count = mask_row.shape[0]
    score_scale = 1.0 / math.sqrt(HD)
    span_ids = jnp.arange(span_count, dtype=jnp.int32)

    def one_block(carry_state, block_index):
        running_max, running_sum, weighted = carry_state
        offset = block_index * length
        key_block = lax.dynamic_slice_in_dim(keys_piece, offset, length, 0).reshape(
            length, heads_dev, HD
        )
        value_block = lax.dynamic_slice_in_dim(values_piece, offset, length, 0).reshape(
            length, heads_dev, HD
        )
        key_span = (offset + jnp.arange(length, dtype=jnp.int32)) // rows_span
        allowed = (
            jnp.sum(jnp.where(key_span[:, None] == span_ids[None, :], mask_row[None, :], 0), axis=1)
            > 0
        )
        scores = (
            jnp.einsum("qhd,khd->hqk", query_block, key_block, preferred_element_type=jnp.float32)
            * score_scale
        )
        scores = jnp.where(allowed[None, None, :], scores, neg_big)
        new_max = jnp.maximum(running_max, jnp.max(scores, axis=2))
        weights = jnp.where(allowed[None, None, :], jnp.exp(scores - new_max[:, :, None]), 0.0)
        factor = jnp.exp(running_max - new_max)
        running_sum = running_sum * factor + jnp.sum(weights, axis=2)
        weighted = weighted * factor.T[:, :, None] + jnp.einsum(
            "hqk,khd->qhd",
            weights.astype(jnp.bfloat16),
            value_block,
            preferred_element_type=jnp.float32,
        )
        return ((new_max, running_sum, weighted), None)

    result, unused = lax.scan(
        one_block, partial_state, jnp.arange(piece_rows // length, dtype=jnp.int32)
    )
    return result


def per_device(
    queries,
    keys,
    values,
    span_mask,
    head_gain,
    head_shift,
    patch_weight,
    noisy_latent,
    conv_weight,
    conv_bias,
):
    heads_dev = queries.shape[1] // HD
    slab_count = lax.axis_size("slab")
    col_dev = TCOLS // slab_count
    slab_place = lax.axis_index("slab")
    span_place = lax.axis_index("span")
    mask_row = lax.dynamic_slice_in_dim(span_mask, span_place, 1, 0)[0]
    token_grid = queries.reshape(FRAMES_SPAN, TROWS, TCOLS, queries.shape[-1])
    picked = lax.dynamic_slice_in_dim(token_grid, slab_place * col_dev, col_dev, 2)
    own_queries = picked.reshape(FRAMES_SPAN * TROWS * col_dev, queries.shape[-1]).reshape(
        -1, heads_dev, HD
    )
    query_rows = own_queries.shape[0]
    rows_span = keys.shape[0] * slab_count
    running_max, running_sum, weighted = fold_keys(
        (
            jnp.full((heads_dev, query_rows), neg_big, jnp.float32),
            jnp.zeros((heads_dev, query_rows), jnp.float32),
            jnp.zeros((query_rows, heads_dev, HD), jnp.float32),
        ),
        (
            lax.all_gather(keys, ("span", "slab"), axis=0, tiled=True),
            lax.all_gather(values, ("span", "slab"), axis=0, tiled=True),
        ),
        own_queries,
        mask_row,
        rows_span,
    )
    attended = (
        (weighted / running_sum.T[:, :, None])
        .astype(jnp.bfloat16)
        .reshape(query_rows, heads_dev * HD)
    )
    feature_width = HEADS * HD
    values32 = attended.astype(jnp.float32)
    row_total = jnp.sum(values32, axis=1)
    row_squares = jnp.sum(values32 * values32, axis=1)
    row_total, row_squares = lax.psum((row_total, row_squares), "head")
    row_mean = row_total / feature_width
    spread = row_squares / feature_width - row_mean * row_mean
    normed = (
        (values32 - row_mean[:, None]) * lax.rsqrt(spread + norm_eps)[:, None] * head_gain[None, :]
        + head_shift[None, :]
    ).astype(jnp.bfloat16)
    normed_grid = normed.reshape(FRAMES_SPAN, TROWS, col_dev, normed.shape[-1])
    own_rows = TROWS // lax.axis_size("head")
    picked = normed_grid
    product = jnp.dot(
        picked.reshape(-1, picked.shape[-1]), patch_weight, preferred_element_type=jnp.float32
    )
    velocity = lax.psum_scatter(
        product.reshape(
            FRAMES_SPAN, own_rows * lax.axis_size("head"), col_dev * patch_weight.shape[1]
        )
        .transpose(1, 0, 2)
        .reshape(own_rows * lax.axis_size("head"), -1)
        .astype(jnp.bfloat16),
        "head",
        scatter_dimension=0,
        tiled=True,
    ).astype(jnp.float32)
    rows_dev = velocity.shape[0]
    patch_cells = (
        velocity.reshape(rows_dev, FRAMES_SPAN, col_dev, 2, 2, LAT_CH)
        .transpose(1, 0, 3, 2, 4, 5)
        .reshape(FRAMES_SPAN, 2 * rows_dev, 2 * col_dev, LAT_CH)
    )
    clean_latent = noisy_latent - noise_level * patch_cells
    latent_input = clean_latent.astype(jnp.bfloat16)
    framed = with_halo(latent_input, (("head", 1), ("slab", 2)), 1)
    earlier = from_behind(framed[FRAMES_SPAN - 2 :], "span", 1)
    stacked = jnp.concatenate([earlier, framed], axis=0)
    height = clean_latent.shape[1]
    breadth = clean_latent.shape[2]
    columns = jnp.concatenate(
        [
            stacked[
                frame_tap : frame_tap + FRAMES_SPAN,
                row_tap : row_tap + height,
                col_tap : col_tap + breadth,
                :,
            ]
            for frame_tap in range(3)
            for row_tap in range(3)
            for col_tap in range(3)
        ],
        axis=-1,
    )
    decoded = (
        jnp.dot(
            columns.reshape(FRAMES_SPAN * height * breadth, 27 * LAT_CH),
            conv_weight,
            preferred_element_type=jnp.float32,
        )
        + conv_bias[None, :]
    )
    decoded = decoded.astype(jnp.bfloat16).reshape(
        FRAMES_SPAN, height, breadth, conv_weight.shape[1]
    )
    return (clean_latent, decoded)


def solution(mesh):
    placed = (
        P(("groups", "span"), "head"),
        P(("groups", "span", "slab"), "head"),
        P(("groups", "span", "slab"), "head"),
        P("groups", None),
        P("head"),
        P("head"),
        P("head", None),
        P(("groups", "span"), "head", "slab", None),
        P(),
        P(),
    )
    return jax.shard_map(
        per_device,
        mesh=mesh,
        in_specs=placed,
        out_specs=(
            P(("groups", "span"), "head", "slab", None),
            P(("groups", "span"), "head", "slab", None),
        ),
        check_vma=False,
    )
```

profile of v0, /device:TPU:0, one launch (start us, length us, event | category | flops | bytes accessed | tf_op | source)
XLA Modules:
  0.0 286.9 jit_solution(14048511079382129699)
XLA Ops:
  8.7 1.0 constant_dynamic-slice_fusion.2
  9.8 1.7 reshape_reshape.3
  11.4 1.2 copy.38
  14.6 75.5 %all-gather.3.cloned.1.call-done = bf16[1536,2560]{1,0:T(8,128)(2,1)} async-done(((bf16[192,2560]{1,0:T(8,128)(2,1)}), bf16[1536,2560]{1,0:T(8,128)(2,1)}) %all-gather.3.cloned.1.call-update) | async-done | bytes 7864336 | tf_op jit(solution)/shard_map/all_gather | solution.py:126
  90.1 78.0 %all-gather.5.cloned.1.call-done = bf16[1536,2560]{1,0:T(8,128)(2,1)} async-done(((bf16[192,2560]{1,0:T(8,128)(2,1)}), bf16[1536,2560]{1,0:T(8,128)(2,1)}) %all-gather.5.cloned.1.call-update) | async-done | bytes 7864336 | tf_op jit(solution)/shard_map/all_gather | solution.py:127
  168.1 70.0 %while.17 = (s32[]{:T(128)}, f32[20,192]{1,0:T(8,128)S(1)}, f32[20,192]{1,0:T(8,128)S(1)}, f32[192,20,128]{2,0,1:T(8,128)}, s32[2]{0:T(128)S(1)}, /*index=5*/s32...) while((s32[]{:T(128)}, f32[20,192]{1,0:T(8,128)S(1)}, ...), condition=%wide.region_4.5_spmd.clone, body=%wide.region_0.4_spmd.clone.sunk | while | flops 1549801728 | bytes 95616248 | solution.py:88
  169.5 7.0 %constant_dynamic-slice_fusion.5 = (bf16[768,2560]{1,0:T(8,128)(2,1)}, bf16[768,2560]{1,0:T(8,128)(2,1)}) fusion(bf16[1536,2560]{1,0:T(8,128)(2,1)} %get-tuple-element.368, s32[]{:T(128)S(6)} %select_n.93, bf16[1536,2560]{1,0:T(8,128)(2,1)} %get-tuple-element.366), kind=kLoop, calls=%fused_computation.26.clone.1 | loop fusion | bytes 15728644 | tf_op jit(solution)/shard_map/while/body/eval_jaxpr/dynamic_slice | solution.py:63
  176.4 6.3 %copy.52 = bf16[768,2560]{0,1:T(8,128)(2,1)} copy(bf16[768,2560]{1,0:T(8,128)(2,1)} %get-tuple-element.328) | data formatting | bytes 7864320 | tf_op jit(solution)/shard_map/while/body/eval_jaxpr/dynamic_slice | solution.py:60
  182.7 6.3 %copy.53 = bf16[768,2560]{0,1:T(8,128)(2,1)} copy(bf16[768,2560]{1,0:T(8,128)(2,1)} %get-tuple-element.332) | data formatting | bytes 7864320 | tf_op jit(solution)/shard_map/while/body/eval_jaxpr/dynamic_slice | solution.py:63
  189.0 4.8 %bitcast_reduce_fusion.2 = (f32[20,192]{1,0:T(8,128)S(1)}, f32[20,768,192]{1,2,0:T(8,128)S(1)}) fusion(pred[768]{0:T(1024)(128)(4,1)S(1)} %broadcast_compare_fusion.2, bf16[192,20,128]{2,0,1:T(8,128)(2,1)} %get-tuple-element.367, bf16[768,20,128]{0,2,1:T(8,128)(2,1)} %bitcast.80), kind=kOutput, calls=%fused_computation.2.clone.1 | convolution fusion | flops 763818240 | bytes 16727808 | tf_op jit(solution)/shard_map/while/body/eval_jaxpr/qhd,khd->hqk/dot_general | solution.py:72
  193.8 4.8 %bitcast_add_fusion.2 = f32[192,20,128]{2,0,1:T(8,128)} fusion(f32[192,20,128]{2,0,1:T(8,128)} %get-tuple-element.350, bf16[768,20,128]{0,2,1:T(8,128)(2,1)S(1)} %bitcast.81, f32[20,768,192]{1,2,0:T(8,128)S(1)} %get-tuple-element.331, f32[20,192]{1,0:T(8,128)S(1)} %get-tuple-element.361, pred[768]{0:T(1024)(128)(4,1)S(1)} %broadcast_compare_fusion.2, ...), kind=kOutput, calls=%fused_computation.11.clone.1 | convolution fusion | flops 771194880 | bytes 19692288 | tf_op jit(solution)/shard_map/while/body/eval_jaxpr/hqk,khd->qhd/dot_general | solution.py:80
  198.6 3.6 %fusion.51 = f32[20,192]{1,0:T(8,128)S(1)} fusion(f32[20,768,192]{1,2,0:T(8,128)S(1)} %get-tuple-element.331, f32[20,192]{1,0:T(8,128)S(1)} %get-tuple-element.361, pred[768]{0:T(1024)(128)(4,1)S(1)} %broadcast_compare_fusion.2), kind=kLoop, calls=%fused_computation.7.clone.1 | loop fusion | flops 14741760 | bytes 11827968 | tf_op jit(solution)/shard_map/while/body/eval_jaxpr/reduce_sum | solution.py:79
  203.7 7.0 %constant_dynamic-slice_fusion.5 = (bf16[768,2560]{1,0:T(8,128)(2,1)}, bf16[768,2560]{1,0:T(8,128)(2,1)}) fusion(bf16[1536,2560]{1,0:T(8,128)(2,1)} %get-tuple-element.368, s32[]{:T(128)S(6)} %select_n.93, bf16[1536,2560]{1,0:T(8,128)(2,1)} %get-tuple-element.366), kind=kLoop, calls=%fused_computation.26.clone.1 | loop fusion | bytes 15728644 | tf_op jit(solution)/shard_map/while/body/eval_jaxpr/dynamic_slice | solution.py:63
  210.6 6.3 %copy.52 = bf16[768,2560]{0,1:T(8,128)(2,1)} copy(bf16[768,2560]{1,0:T(8,128)(2,1)} %get-tuple-element.328) | data formatting | bytes 7864320 | tf_op jit(solution)/shard_map/while/body/eval_jaxpr/dynamic_slice | solution.py:60
  216.9 6.3 %copy.53 = bf16[768,2560]{0,1:T(8,128)(2,1)} copy(bf16[768,2560]{1,0:T(8,128)(2,1)} %get-tuple-element.332) | data formatting | bytes 7864320 | tf_op jit(solution)/shard_map/while/body/eval_jaxpr/dynamic_slice | solution.py:63
  223.2 4.8 %bitcast_reduce_fusion.2 = (f32[20,192]{1,0:T(8,128)S(1)}, f32[20,768,192]{1,2,0:T(8,128)S(1)}) fusion(pred[768]{0:T(1024)(128)(4,1)S(1)} %broadcast_compare_fusion.2, bf16[192,20,128]{2,0,1:T(8,128)(2,1)} %get-tuple-element.367, bf16[768,20,128]{0,2,1:T(8,128)(2,1)} %bitcast.80), kind=kOutput, calls=%fused_computation.2.clone.1 | convolution fusion | flops 763818240 | bytes 16727808 | tf_op jit(solution)/shard_map/while/body/eval_jaxpr/qhd,khd->hqk/dot_general | solution.py:72
  228.0 6.4 %bitcast_add_fusion.2 = f32[192,20,128]{2,0,1:T(8,128)} fusion(f32[192,20,128]{2,0,1:T(8,128)} %get-tuple-element.350, bf16[768,20,128]{0,2,1:T(8,128)(2,1)S(1)} %bitcast.81, f32[20,768,192]{1,2,0:T(8,128)S(1)} %get-tuple-element.331, f32[20,192]{1,0:T(8,128)S(1)} %get-tuple-element.361, pred[768]{0:T(1024)(128)(4,1)S(1)} %broadcast_compare_fusion.2, ...), kind=kOutput, calls=%fused_computation.11.clone.1 | convolution fusion | flops 771194880 | bytes 19692288 | tf_op jit(solution)/shard_map/while/body/eval_jaxpr/hqk,khd->qhd/dot_general | solution.py:80
  234.4 3.6 %fusion.51 = f32[20,192]{1,0:T(8,128)S(1)} fusion(f32[20,768,192]{1,2,0:T(8,128)S(1)} %get-tuple-element.331, f32[20,192]{1,0:T(8,128)S(1)} %get-tuple-element.361, pred[768]{0:T(1024)(128)(4,1)S(1)} %broadcast_compare_fusion.2), kind=kLoop, calls=%fused_computation.7.clone.1 | loop fusion | flops 14741760 | bytes 11827968 | tf_op jit(solution)/shard_map/while/body/eval_jaxpr/reduce_sum | solution.py:79
  238.1 2.2 convert_reduce_fusion
  240.4 4.9 %all-reduce.1 = (f32[192]{0:T(256)S(1)}, f32[192]{0:T(256)S(1)}) all-reduce(f32[192]{0:T(256)S(1)} %get-tuple-element.200, f32[192]{0:T(256)S(1)} %get-tuple-element.199), channel_id=1, replica_groups=mesh['groups'=2,'span'=4,'head'=2,'slab'=2] {'head'}, use_global_device_ids=true, to_apply=%region_8.9 | all-reduce | flops 384 | bytes 3072 | tf_op jit(solution)/shard_map/psum | solution.py:142
  245.3 1.6 convolution_convert_fusion
  247.1 8.3 %all-reduce = bf16[8,1536]{1,0:T(8,128)(2,1)S(1)} all-reduce(bf16[8,1536]{1,0:T(8,128)(2,1)S(1)} %bitcast.86), channel_id=2, replica_groups=mesh['groups'=2,'span'=4,'head'=2,'slab'=2] {'head'}, use_global_device_ids=true, to_apply=%region_9.10.clone | all-reduce | flops 12288 | bytes 49152
  256.6 2.4 collective-permute-start
  259.0 1.3 collective-permute-start.1
  260.4 4.2 %collective-permute-done.1 = bf16[3,1,16,16]{3,2,1,0:T(8,128)(2,1)S(1)} collective-permute-done((bf16[3,1,16,16]{3,2,1,0:T(8,128)(2,1)S(1)}, bf16[3,1,16,16]{3,2,1,0:T(8,128)(2,1)S(1)}, u32[]{:S(2)}, u32[]{:S(2)}) %collective-permute-start.1) | collective-permute-done | bytes 1568 | tf_op jit(solution)/shard_map/ppermute | solution.py:28
  264.6 1.3 collective-permute-start.2
  265.9 1.3 collective-permute-start.3
  267.9 1.1 collective-permute-done.3
  269.1 1.3 collective-permute-start.4
  271.3 2.2 collective-permute-done.4
  274.6 3.2 %concatenate.35 = bf16[3,8,16,432]{3,2,1,0:T(8,128)(2,1)} concatenate(bf16[3,8,16,16]{3,2,1,0:T(8,128)(2,1)} %get-tuple-element.247, bf16[3,8,16,16]{3,2,1,0:T(8,128)(2,1)} %get-tuple-element.246, bf16[3,8,16,16]{3,2,1,0:T(8,128)(2,1)} %get-tuple-element.245, bf16[3,8,16,16]{3,2,1,0:T(8,128)(2,1)S(1)} %get-tuple-element.244, bf16[3,8,16,16]{3,2,1,0:T(8,128)(2,1)S(1)} %get-tuple-element.243, ...), dimensions={3} | concatenate | bytes 663552 | tf_op jit(solution)/shard_map/concatenate | solution.py:179
  277.8 2.2 fusion.23
  (57 shorter events, 8.5 us)
Async XLA Ops:
  7.2 1.6 copy-start
  7.2 5.5 %copy-start.6 = (u32[32]{0:T(128)S(1)}, u32[32]{0:T(128)}, u32[]{:S(2)}) copy-start(u32[32]{0:T(128)} %constant.95) | copy-start | bytes 388
  7.2 82.9 %all-gather.3.cloned.1.call-start = ((), (), s32[]{:S(2)}) async-start(), calls=%async_computation | async-start | bytes 8847360 | tf_op jit(solution)/shard_map/all_gather | solution.py:126
  7.9 160.2 %all-gather.5.cloned.1.call-start = ((), (), s32[]{:S(2)}) async-start(), calls=%async_computation.1 | async-start | bytes 8847360 | tf_op jit(solution)/shard_map/all_gather | solution.py:127
  168.1 77.2 %copy-start.3 = (f32[2560]{0:T(1024)S(1)}, f32[2560]{0:T(1024)}, u32[]{:S(2)}) copy-start(f32[2560]{0:T(1024)} %param.17) | copy-start | bytes 30724
  168.1 77.2 %copy-start.4 = (f32[2560]{0:T(1024)S(1)}, f32[2560]{0:T(1024)}, u32[]{:S(2)}) copy-start(f32[2560]{0:T(1024)} %param.16) | copy-start | bytes 30724
  189.0 4.8 %copy-start.1 = (bf16[768,2560]{0,1:T(8,128)(2,1)S(1)}, bf16[768,2560]{0,1:T(8,128)(2,1)}, u32[]{:S(2)}) copy-start(bf16[768,2560]{0,1:T(8,128)(2,1)} %copy.53) | copy-start | bytes 11796484 | tf_op jit(solution)/shard_map/while
  223.2 4.8 %copy-start.1 = (bf16[768,2560]{0,1:T(8,128)(2,1)S(1)}, bf16[768,2560]{0,1:T(8,128)(2,1)}, u32[]{:S(2)}) copy-start(bf16[768,2560]{0,1:T(8,128)(2,1)} %copy.53) | copy-start | bytes 11796484 | tf_op jit(solution)/shard_map/while
  238.1 17.7 %copy-start.2 = (f32[3,8,16,16]{3,2,1,0:T(8,128)S(1)}, f32[3,8,16,16]{3,2,1,0:T(8,128)}, u32[]{:S(2)}) copy-start(f32[3,8,16,16]{3,2,1,0:T(8,128)} %param.19) | copy-start | bytes 73732
  256.6 3.8 %collective-permute-start = (bf16[3,1,16,16]{3,2,1,0:T(8,128)(2,1)S(1)}, bf16[3,1,16,16]{3,2,1,0:T(8,128)(2,1)S(1)}, u32[]{:S(2)}, u32[]{:S(2)}) collective-permute-start(bf16[3,1,16,16]{3,2,1,0:T(8,128)(2,1)S(1)} %get-tuple-element.260), channel_id=1, source_target_pairs={{0,2},{1,3},{4,6},{5,7},{8,10},{9,11},{12,14},{13,15},{16,18},{17,... | collective-permute-start | bytes 4616 | tf_op jit(solution)/shard_map/ppermute | solution.py:26
  259.0 5.6 %collective-permute-start.1 = (bf16[3,1,16,16]{3,2,1,0:T(8,128)(2,1)S(1)}, bf16[3,1,16,16]{3,2,1,0:T(8,128)(2,1)S(1)}, u32[]{:S(2)}, u32[]{:S(2)}) collective-permute-start(bf16[3,1,16,16]{3,2,1,0:T(8,128)(2,1)S(1)} %get-tuple-element.261), channel_id=1, source_target_pairs={{2,0},{3,1},{6,4},{7,5},{10,8},{11,9},{14,12},{15,13},{18,16},{19,... | collective-permute-start | bytes 4616 | tf_op jit(solution)/shard_map/ppermute | solution.py:28
  264.6 3.3 %collective-permute-start.2 = (bf16[3,10,1,16]{3,2,1,0:T(2,128)(2,1)S(1)}, bf16[3,10,1,16]{3,2,1,0:T(2,128)(2,1)S(1)}, u32[]{:S(2)}, u32[]{:S(2)}) collective-permute-start(bf16[3,10,1,16]{3,2,1,0:T(2,128)(2,1)S(1)} %get-tuple-element.256), channel_id=1, source_target_pairs={{0,1},{2,3},{4,5},{6,7},{8,9},{10,11},{12,13},{14,15},{16,17},{18,... | collective-permute-start | bytes 2888 | tf_op jit(solution)/shard_map/ppermute | solution.py:26
  265.9 3.1 %collective-permute-start.3 = (bf16[3,10,1,16]{3,2,1,0:T(2,128)(2,1)S(1)}, bf16[3,10,1,16]{3,2,1,0:T(2,128)(2,1)S(1)}, u32[]{:S(2)}, u32[]{:S(2)}) collective-permute-start(bf16[3,10,1,16]{3,2,1,0:T(2,128)(2,1)S(1)} %get-tuple-element.257), channel_id=1, source_target_pairs={{1,0},{3,2},{5,4},{7,6},{9,8},{11,10},{13,12},{15,14},{17,16},{19,... | collective-permute-start | bytes 2888 | tf_op jit(solution)/shard_map/ppermute | solution.py:28
  269.1 4.5 %collective-permute-start.4 = (bf16[2,10,18,16]{3,2,1,0:T(8,128)(2,1)S(1)}, bf16[2,10,18,16]{3,2,1,0:T(8,128)(2,1)S(1)}, u32[]{:S(2)}, u32[]{:S(2)}) collective-permute-start(bf16[2,10,18,16]{3,2,1,0:T(8,128)(2,1)S(1)} %pad_maximum_fusion.1), channel_id=1, source_target_pairs={{0,4},{4,8},{8,12},{1,5},{5,9},{9,13},{2,6},{6,10},{10,14},{3,7},{... | collective-permute-start | bytes 34568 | tf_op jit(solution)/shard_map/ppermute | solution.py:38
  270.5 7.4 %copy-start.5 = (f32[384]{0:T(512)S(1)}, f32[384]{0:T(512)}, u32[]{:S(2)}) copy-start(f32[384]{0:T(512)} %param.21) | copy-start | bytes 4612
Sparse Core Ops, SparseCore 0:
  9.7 80.4 all-gather.2
  91.8 76.2 all-gather.4
where the time goes:
time: 288 us; the launch traced here: 287 us
  waiting for transfers between devices  162 us (56%)
  local copies, waits for them, and re-layouts  51.2 us (18%)
  matrix products  24.5 us (9%)
  between operations  14.9 us (5%)
  blocking collectives  13.3 us (5%)
  other arithmetic  11.5 us (4%)
  starting transfers between devices  7.64 us (3%)
    all_gather x1, waiting for transfers between devices, per_device(): lax.all_gather(values, ('span', 'slab'), axis=0, tiled=True)  78 us
    all_gather x1, waiting for transfers between devices, per_device(): lax.all_gather(keys, ('span', 'slab'), axis=0, tiled=True)  75.5 us
    dynamic_slice x4, local copies, waits for them, and re-layouts, one_block(): lax.dynamic_slice_in_dim(values_piece, offset, length, 0)  26.6 us
    dynamic_slice x2, local copies, waits for them, and re-layouts, one_block(): lax.dynamic_slice_in_dim(keys_piece, offset, length, 0)  12.6 us
    dot_general x2, matrix products, one_block(): jnp.einsum('hqk,khd->qhd', weights.astype(jnp.bfloat16), value_block, pre...  11.2 us
    dot_general x2, matrix products, one_block(): jnp.einsum('qhd,khd->hqk', query_block, key_block, preferred_element_type...  9.52 us
    unnamed x1, blocking collectives  8.32 us
    reduce_sum x2, other arithmetic, one_block(): running_sum = running_sum * factor + jnp.sum(weights, axis=2)  7.25 us
  transfers between devices with their start and end apart: 7, of which 6 were waited for; matrix products, arithmetic and copies ran while one was open for 2% of the time, Pallas kernels for 0%

commit v1 on v0

--- a/solution.py
+++ b/solution.py
@@ -1,3 +1,4 @@
+import functools
 import math
 import jax
 import jax.numpy as jnp
@@ -13,6 +14,34 @@
 neg_big = -1e30
 noise_level = 0.75
 norm_eps = 1e-06
+
+
+def create_tasks_for(matrix, ax_name):
+    moved = jax.lax.axis_size(ax_name)
+    row_out = jax.lax.axis_index(ax_name)
+    v1, part_now, part_next = (moved, row_out, matrix.shape[0])
+    made = tuple(((nth, (nth + 1) % v1) for nth in range(v1)))
+    line_up = tuple(((nth, (nth - 1) % v1) for nth in range(v1)))
+    answer = jnp.zeros((*matrix.shape[:0], v1 * part_next, *matrix.shape[1:]), matrix.dtype)
+    arr_next = parts_out = matrix
+    f_now = v1 // 2
+    dev_j = 1
+    answer = lax.dynamic_update_slice_in_dim(answer, matrix, part_now * part_next, axis=0)
+    while dev_j < f_now + 1:
+        arr_next = jax.lax.ppermute(arr_next, axis_name=ax_name, perm=made)
+        answer = lax.dynamic_update_slice_in_dim(
+            answer, arr_next, (part_now - dev_j) % v1 * part_next, axis=0
+        )
+        if dev_j < v1 - f_now:
+            parts_out = jax.lax.ppermute(parts_out, axis_name=ax_name, perm=line_up)
+            answer = lax.dynamic_update_slice_in_dim(
+                answer, parts_out, (part_now + dev_j) % v1 * part_next, axis=0
+            )
+        dev_j += 1
+    return answer
+
+
+_create_words = functools.partial(create_tasks_for, ax_name=("span", "slab"))
 
 
 def with_halo(cells, sides, width):
@@ -122,10 +151,7 @@
             jnp.zeros((heads_dev, query_rows), jnp.float32),
             jnp.zeros((query_rows, heads_dev, HD), jnp.float32),
         ),
-        (
-            lax.all_gather(keys, ("span", "slab"), axis=0, tiled=True),
-            lax.all_gather(values, ("span", "slab"), axis=0, tiled=True),
-        ),
+        (_create_words(keys), lax.all_gather(values, ("span", "slab"), axis=0, tiled=True)),
         own_queries,
         mask_row,
         rows_span,

time: 288 us -> 373 us (1.30)
  local copies, waits for them, and re-layouts: 51.2 us -> 160 us
  waiting for transfers between devices: 162 us -> 107 us
  starting transfers between devices: 7.64 us -> 41.8 us
  matrix products: 24.5 us -> 18.7 us
    dynamic_update_slice x0 -> x8, local copies, waits for them, and re-layouts: none -> 105 us  [the longest x4 51.8 us: create_tasks_for(): lax.dynamic_update_slice_in_dim(answer, arr_next, (part_now - dev_j) % v1...]
    ppermute x0 -> x7, waiting for transfers between devices: none -> 99.1 us  [the longest x4 80.1 us: create_tasks_for(): arr_next = jax.lax.ppermute(arr_next, axis_name=ax_name, perm=made)]
    all_gather x1, waiting for transfers between devices: 78 us -> 0.01 us  [per_device(): lax.all_gather(values, ('span', 'slab'), axis=0, tiled=True)]
    all_gather x1 -> x0, waiting for transfers between devices: 75.5 us -> none  [per_device(): lax.all_gather(keys, ('span', 'slab'), axis=0, tiled=True)]
    ppermute x0 -> x7, starting transfers between devices: none -> 21.8 us  [the longest x3 11.6 us: create_tasks_for(): parts_out = jax.lax.ppermute(parts_out, axis_name=ax_name, perm=line_up)]
    ppermute x1, starting transfers between devices: 1.3 us -> 14.2 us  [from_behind(): return lax.ppermute(value, axis, pairs)]
    ppermute x0 -> x7, local copies, waits for them, and re-layouts: none -> 9.77 us  [the longest x4 6.13 us: create_tasks_for(): arr_next = jax.lax.ppermute(arr_next, axis_name=ax_name, perm=made)]
    dynamic_slice x2, local copies, waits for them, and re-layouts: 12.6 us -> 4.73 us  [one_block(): lax.dynamic_slice_in_dim(keys_piece, offset, length, 0)]
  transfers between devices with their start and end apart: 7 -> 13, of which waited for: 6 -> 9; matrix products, arithmetic and copies ran while one was open for 2% -> 35% of each run, Pallas kernels for 0% -> 0%
where the time goes in v1:
time: 373 us; the launch traced here: 369 us
  local copies, waits for them, and re-layouts  160 us (43%)
  waiting for transfers between devices  107 us (29%)
  starting transfers between devices  41.8 us (11%)
  matrix products  18.7 us (5%)
  between operations  15 us (4%)
  blocking collectives  13.9 us (4%)
  other arithmetic  11.5 us (3%)
    ppermute x4, waiting for transfers between devices, create_tasks_for(): arr_next = jax.lax.ppermute(arr_next, axis_name=ax_name, perm=made)  80.1 us
    dynamic_update_slice x4, local copies, waits for them, and re-layouts, create_tasks_for(): lax.dynamic_update_slice_in_dim(answer, arr_next, (part_now - dev_j) % v1...  51.8 us
    dynamic_update_slice x3, local copies, waits for them, and re-layouts, create_tasks_for(): lax.dynamic_update_slice_in_dim(answer, parts_out, (part_now + dev_j) % v...  40.5 us
    dynamic_slice x4, local copies, waits for them, and re-layouts, one_block(): lax.dynamic_slice_in_dim(values_piece, offset, length, 0)  21 us
    ppermute x3, waiting for transfers between devices, create_tasks_for(): parts_out = jax.lax.ppermute(parts_out, axis_name=ax_name, perm=line_up)  18.9 us
    ppermute x1, starting transfers between devices, from_behind(): return lax.ppermute(value, axis, pairs)  14.2 us
    dynamic_update_slice x1, local copies, waits for them, and re-layouts, create_tasks_for(): lax.dynamic_update_slice_in_dim(answer, matrix, part_now * part_next, axi...  12.6 us
    ppermute x3, starting transfers between devices, create_tasks_for(): parts_out = jax.lax.ppermute(parts_out, axis_name=ax_name, perm=line_up)  11.6 us
  transfers between devices with their start and end apart: 13, of which 9 were waited for; matrix products, arithmetic and copies ran while one was open for 35% of the time, Pallas kernels for 0%

profile of v1, /device:TPU:0, one launch (start us, length us, event | category | flops | bytes accessed | tf_op | source)
XLA Modules:
  0.0 369.2 jit_solution(13091725520436589946)
XLA Ops:
  8.4 4.1 %collective-permute-start.1 = (bf16[192,2560]{1,0:T(8,128)(2,1)}, bf16[192,2560]{1,0:T(8,128)(2,1)S(1)}, u32[]{:S(2)}, u32[]{:S(2)}) collective-permute-start(bf16[192,2560]{1,0:T(8,128)(2,1)} %param.13), channel_id=1, source_target_pairs={{0,13},{1,0},{4,1},{5,4},{8,5},{9,8},{12,9},{13,12},{2,15},{3,2},{... | collective-permute-start | bytes 2949128 | tf_op jit(solution)/shard_map/ppermute | solution.py:36
  12.5 26.8 %collective-permute-done = bf16[192,2560]{1,0:T(8,128)(2,1)S(1)} collective-permute-done((bf16[192,2560]{1,0:T(8,128)(2,1)}, bf16[192,2560]{1,0:T(8,128)(2,1)S(1)}, u32[]{:S(2)}, u32[]{:S(2)}) %collective-permute-start) | collective-permute-done | bytes 983072 | tf_op jit(solution)/shard_map/ppermute | solution.py:31
  40.2 7.6 %collective-permute-done.1 = bf16[192,2560]{1,0:T(8,128)(2,1)S(1)} collective-permute-done((bf16[192,2560]{1,0:T(8,128)(2,1)}, bf16[192,2560]{1,0:T(8,128)(2,1)S(1)}, u32[]{:S(2)}, u32[]{:S(2)}) %collective-permute-start.1) | collective-permute-done | bytes 983072 | tf_op jit(solution)/shard_map/ppermute | solution.py:36
  48.7 3.6 collective-permute-start.3
  52.4 29.5 %collective-permute-done.2 = bf16[192,2560]{1,0:T(8,128)(2,1)S(1)} collective-permute-done((bf16[192,2560]{1,0:T(8,128)(2,1)S(1)}, bf16[192,2560]{1,0:T(8,128)(2,1)S(1)}, u32[]{:S(2)}, u32[]{:S(2)}) %collective-permute-start.2) | collective-permute-done | bytes 983072 | tf_op jit(solution)/shard_map/ppermute | solution.py:31
  83.2 11.3 %collective-permute-done.3 = bf16[192,2560]{1,0:T(8,128)(2,1)} collective-permute-done((bf16[192,2560]{1,0:T(8,128)(2,1)S(1)}, bf16[192,2560]{1,0:T(8,128)(2,1)}, u32[]{:S(2)}, u32[]{:S(2)}) %collective-permute-start.3) | collective-permute-done | bytes 983072 | tf_op jit(solution)/shard_map/ppermute | solution.py:36
  94.5 3.8 %collective-permute-start.5 = (bf16[192,2560]{1,0:T(8,128)(2,1)}, bf16[192,2560]{1,0:T(8,128)(2,1)}, u32[]{:S(2)}, u32[]{:S(2)}) collective-permute-start(bf16[192,2560]{1,0:T(8,128)(2,1)} %collective-permute-done.3), channel_id=1, source_target_pairs={{0,13},{1,0},{4,1},{5,4},{8,5},{9,8},{12,9},{13,12},{2,15},{3,2},{... | collective-permute-start | bytes 2949128 | tf_op jit(solution)/shard_map/ppermute | solution.py:36
  98.4 23.8 %collective-permute-done.4 = bf16[192,2560]{1,0:T(8,128)(2,1)} collective-permute-done((bf16[192,2560]{1,0:T(8,128)(2,1)S(1)}, bf16[192,2560]{1,0:T(8,128)(2,1)}, u32[]{:S(2)}, u32[]{:S(2)}) %collective-permute-start.4) | collective-permute-done | bytes 983072 | tf_op jit(solution)/shard_map/ppermute | solution.py:31
  122.2 7.6 %collective-permute-start.6 = (bf16[192,2560]{1,0:T(8,128)(2,1)}, bf16[192,2560]{1,0:T(8,128)(2,1)}, u32[]{:S(2)}, u32[]{:S(2)}) collective-permute-start(bf16[192,2560]{1,0:T(8,128)(2,1)} %collective-permute-done.4), channel_id=1, source_target_pairs={{0,1},{1,4},{4,5},{5,8},{8,9},{9,12},{12,13},{13,0},{2,3},{3,6},{6... | collective-permute-start | bytes 2949128 | tf_op jit(solution)/shard_map/ppermute | solution.py:31
  137.7 3.7 broadcast_in_dim.80
  141.3 12.6 %dynamic_update_slice.24 = bf16[1536,2560]{0,1:T(8,128)(2,1)} dynamic-update-slice(bf16[1536,2560]{0,1:T(8,128)(2,1)} %broadcast_in_dim.80, bf16[192,2560]{0,1:T(8,128)(2,1)S(1)} %copy.48, s32[]{:T(128)S(6)} %select_n.104, s32[]{:T(128)} %constant.123.clone.1) | dynamic-update-slice | bytes 1966084 | tf_op jit(solution)/shard_map/dynamic_update_slice | solution.py:29
  156.2 13.2 %dynamic_update_slice.25 = bf16[1536,2560]{0,1:T(8,128)(2,1)} dynamic-update-slice(bf16[1536,2560]{0,1:T(8,128)(2,1)} %dynamic_update_slice.24, bf16[192,2560]{0,1:T(8,128)(2,1)S(1)} %copy.49, s32[]{:T(128)S(6)} %select_n.106, s32[]{:T(128)} %constant.123.clone.1) | dynamic-update-slice | bytes 1966084 | tf_op jit(solution)/shard_map/dynamic_update_slice | solution.py:32
  170.0 14.0 %dynamic_update_slice.26 = bf16[1536,2560]{0,1:T(8,128)(2,1)} dynamic-update-slice(bf16[1536,2560]{0,1:T(8,128)(2,1)} %dynamic_update_slice.25, bf16[192,2560]{0,1:T(8,128)(2,1)S(1)} %copy.50, s32[]{:T(128)S(6)} %select_n.108, s32[]{:T(128)} %constant.123.clone.1) | dynamic-update-slice | bytes 1966084 | tf_op jit(solution)/shard_map/dynamic_update_slice | solution.py:37
  185.5 12.2 %dynamic_update_slice.27 = bf16[1536,2560]{0,1:T(8,128)(2,1)} dynamic-update-slice(bf16[1536,2560]{0,1:T(8,128)(2,1)} %dynamic_update_slice.26, bf16[192,2560]{0,1:T(8,128)(2,1)S(1)} %copy.51, s32[]{:T(128)S(6)} %select_n.110, s32[]{:T(128)} %constant.123.clone.1) | dynamic-update-slice | bytes 1966084 | tf_op jit(solution)/shard_map/dynamic_update_slice | solution.py:32
  199.2 12.5 %dynamic_update_slice.28 = bf16[1536,2560]{0,1:T(8,128)(2,1)} dynamic-update-slice(bf16[1536,2560]{0,1:T(8,128)(2,1)} %dynamic_update_slice.27, bf16[192,2560]{0,1:T(8,128)(2,1)S(1)} %copy.52, s32[]{:T(128)S(6)} %select_n.112, s32[]{:T(128)} %constant.123.clone.1) | dynamic-update-slice | bytes 1966084 | tf_op jit(solution)/shard_map/dynamic_update_slice | solution.py:37
  213.3 14.0 %dynamic_update_slice.29 = bf16[1536,2560]{0,1:T(8,128)(2,1)} dynamic-update-slice(bf16[1536,2560]{0,1:T(8,128)(2,1)} %dynamic_update_slice.28, bf16[192,2560]{0,1:T(8,128)(2,1)S(1)} %copy.53, s32[]{:T(128)S(6)} %select_n.114, s32[]{:T(128)} %constant.123.clone.1) | dynamic-update-slice | bytes 1966084 | tf_op jit(solution)/shard_map/dynamic_update_slice | solution.py:32
  228.8 14.0 %dynamic_update_slice.30 = bf16[1536,2560]{0,1:T(8,128)(2,1)} dynamic-update-slice(bf16[1536,2560]{0,1:T(8,128)(2,1)} %dynamic_update_slice.29, bf16[192,2560]{0,1:T(8,128)(2,1)S(1)} %copy.54, s32[]{:T(128)S(6)} %select_n.116, s32[]{:T(128)} %constant.123.clone.1) | dynamic-update-slice | bytes 1966084 | tf_op jit(solution)/shard_map/dynamic_update_slice | solution.py:37
  244.3 12.5 %dynamic_update_slice.31 = bf16[1536,2560]{0,1:T(8,128)(2,1)} dynamic-update-slice(bf16[1536,2560]{0,1:T(8,128)(2,1)} %dynamic_update_slice.30, bf16[192,2560]{0,1:T(8,128)(2,1)S(1)} %copy.55, s32[]{:T(128)S(6)} %select_n.118, s32[]{:T(128)} %constant.123.clone.1) | dynamic-update-slice | bytes 1966084 | tf_op jit(solution)/shard_map/dynamic_update_slice | solution.py:32
  256.8 51.8 %while.17 = (s32[]{:T(128)}, f32[20,192]{1,0:T(8,128)S(1)}, f32[20,192]{1,0:T(8,128)S(1)}, f32[192,20,128]{2,0,1:T(8,128)}, s32[2]{0:T(128)S(1)}, /*index=5*/s32...) while((s32[]{:T(128)}, f32[20,192]{1,0:T(8,128)S(1)}, ...), condition=%wide.region_4.5_spmd.clone, body=%wide.region_0.4_spmd.clone.sunk | while | flops 1549801728 | bytes 87751936 | solution.py:117
  258.2 4.2 %constant_dynamic-slice_fusion.7 = bf16[768,2560]{1,0:T(8,128)(2,1)} fusion(bf16[1536,2560]{1,0:T(8,128)(2,1)} %get-tuple-element.362, s32[]{:T(128)S(6)} %select_n.163), kind=kLoop, calls=%fused_computation.26.clone.1 | loop fusion | bytes 7864324 | tf_op jit(solution)/shard_map/while/body/eval_jaxpr/dynamic_slice | solution.py:92
  262.4 6.3 %copy.68 = bf16[768,2560]{0,1:T(8,128)(2,1)} copy(bf16[768,2560]{1,0:T(8,128)(2,1)} %constant_dynamic-slice_fusion.7) | data formatting | bytes 7864320 | tf_op jit(solution)/shard_map/while/body/eval_jaxpr/dynamic_slice | solution.py:92
  273.4 4.8 %bitcast_add_fusion.2 = f32[192,20,128]{2,0,1:T(8,128)} fusion(f32[192,20,128]{2,0,1:T(8,128)} %get-tuple-element.344, bf16[768,20,128]{0,2,1:T(8,128)(2,1)S(1)} %bitcast.81, f32[20,768,192]{1,2,0:T(8,128)S(1)} %get-tuple-element.326, f32[20,192]{1,0:T(8,128)S(1)} %get-tuple-element.355, pred[768]{0:T(1024)(128)(4,1)S(1)} %broadcast_compare_fusion.2, ...), kind=kOutput, calls=%fused_computation.11.clone.1 | convolution fusion | flops 771194880 | bytes 19692288 | tf_op jit(solution)/shard_map/while/body/eval_jaxpr/hqk,khd->qhd/dot_general | solution.py:109
  278.2 3.6 fusion.51
  283.2 4.2 %constant_dynamic-slice_fusion.7 = bf16[768,2560]{1,0:T(8,128)(2,1)} fusion(bf16[1536,2560]{1,0:T(8,128)(2,1)} %get-tuple-element.362, s32[]{:T(128)S(6)} %select_n.163), kind=kLoop, calls=%fused_computation.26.clone.1 | loop fusion | bytes 7864324 | tf_op jit(solution)/shard_map/while/body/eval_jaxpr/dynamic_slice | solution.py:92
  287.5 6.3 %copy.68 = bf16[768,2560]{0,1:T(8,128)(2,1)} copy(bf16[768,2560]{1,0:T(8,128)(2,1)} %constant_dynamic-slice_fusion.7) | data formatting | bytes 7864320 | tf_op jit(solution)/shard_map/while/body/eval_jaxpr/dynamic_slice | solution.py:92
  298.5 6.5 %bitcast_add_fusion.2 = f32[192,20,128]{2,0,1:T(8,128)} fusion(f32[192,20,128]{2,0,1:T(8,128)} %get-tuple-element.344, bf16[768,20,128]{0,2,1:T(8,128)(2,1)S(1)} %bitcast.81, f32[20,768,192]{1,2,0:T(8,128)S(1)} %get-tuple-element.326, f32[20,192]{1,0:T(8,128)S(1)} %get-tuple-element.355, pred[768]{0:T(1024)(128)(4,1)S(1)} %broadcast_compare_fusion.2, ...), kind=kOutput, calls=%fused_computation.11.clone.1 | convolution fusion | flops 771194880 | bytes 19692288 | tf_op jit(solution)/shard_map/while/body/eval_jaxpr/hqk,khd->qhd/dot_general | solution.py:109
  304.9 3.6 fusion.51
  310.8 5.1 %all-reduce.1 = (f32[192]{0:T(256)S(1)}, f32[192]{0:T(256)S(1)}) all-reduce(f32[192]{0:T(256)S(1)} %get-tuple-element.200, f32[192]{0:T(256)S(1)} %get-tuple-element.199), channel_id=1, replica_groups=mesh['groups'=2,'span'=4,'head'=2,'slab'=2] {'head'}, use_global_device_ids=true, to_apply=%region_8.9 | all-reduce | flops 384 | bytes 3072 | tf_op jit(solution)/shard_map/psum | solution.py:168
  316.8 8.8 %all-reduce = bf16[8,1536]{1,0:T(8,128)(2,1)S(1)} all-reduce(bf16[8,1536]{1,0:T(8,128)(2,1)S(1)} %bitcast.86), channel_id=2, replica_groups=mesh['groups'=2,'span'=4,'head'=2,'slab'=2] {'head'}, use_global_device_ids=true, to_apply=%region_9.10.clone | all-reduce | flops 12288 | bytes 49152
  330.1 4.2 %collective-permute-done.8 = bf16[3,1,16,16]{3,2,1,0:T(8,128)(2,1)S(1)} collective-permute-done((bf16[3,1,16,16]{3,2,1,0:T(8,128)(2,1)S(1)}, bf16[3,1,16,16]{3,2,1,0:T(8,128)(2,1)S(1)}, u32[]{:S(2)}, u32[]{:S(2)}) %collective-permute-start.8) | collective-permute-done | bytes 1568 | tf_op jit(solution)/shard_map/ppermute | solution.py:57
  338.8 14.2 %collective-permute-start.11 = (bf16[2,10,18,16]{3,2,1,0:T(8,128)(2,1)S(1)}, bf16[2,10,18,16]{3,2,1,0:T(8,128)(2,1)S(1)}, u32[]{:S(2)}, u32[]{:S(2)}) collective-permute-start(bf16[2,10,18,16]{3,2,1,0:T(8,128)(2,1)S(1)} %pad_maximum_fusion.1), channel_id=1, source_target_pairs={{0,4},{4,8},{8,12},{1,5},{5,9},{9,13},{2,6},{6,10},{10,14},{3,7},{... | collective-permute-start | bytes 34568 | tf_op jit(solution)/shard_map/ppermute | solution.py:67
  356.9 3.2 concatenate.35
  (97 shorter events, 50.9 us)
Async XLA Ops:
  7.2 124.2 %copy-start = (bf16[384,2560]{1,0:T(8,128)(2,1)S(1)}, bf16[384,2560]{1,0:T(8,128)(2,1)}, u32[]{:S(2)}) copy-start(bf16[384,2560]{1,0:T(8,128)(2,1)} %param.12) | copy-start | bytes 5898244
  7.2 249.6 %all-gather.2.cloned.1.call-start = ((), (), s32[]{:S(2)}) async-start(), calls=%async_computation | async-start | bytes 8847360 | tf_op jit(solution)/shard_map/all_gather | solution.py:154
  7.9 31.5 %collective-permute-start = (bf16[192,2560]{1,0:T(8,128)(2,1)}, bf16[192,2560]{1,0:T(8,128)(2,1)S(1)}, u32[]{:S(2)}, u32[]{:S(2)}) collective-permute-start(bf16[192,2560]{1,0:T(8,128)(2,1)} %param.13), channel_id=1, source_target_pairs={{0,1},{1,4},{4,5},{5,8},{8,9},{9,12},{12,13},{13,0},{2,3},{3,6},{6... | collective-permute-start | bytes 2949128 | tf_op jit(solution)/shard_map/ppermute | solution.py:31
  8.4 39.3 %collective-permute-start.1 = (bf16[192,2560]{1,0:T(8,128)(2,1)}, bf16[192,2560]{1,0:T(8,128)(2,1)S(1)}, u32[]{:S(2)}, u32[]{:S(2)}) collective-permute-start(bf16[192,2560]{1,0:T(8,128)(2,1)} %param.13), channel_id=1, source_target_pairs={{0,13},{1,0},{4,1},{5,4},{8,5},{9,8},{12,9},{13,12},{2,15},{3,2},{... | collective-permute-start | bytes 2949128 | tf_op jit(solution)/shard_map/ppermute | solution.py:36
  39.4 82.8 %copy-start.6 = (bf16[192,2560]{1,0:T(8,128)(2,1)}, bf16[192,2560]{1,0:T(8,128)(2,1)S(1)}, u32[]{:S(2)}) copy-start(bf16[192,2560]{1,0:T(8,128)(2,1)S(1)} %collective-permute-done) | copy-start | bytes 2949124
  39.4 42.5 %collective-permute-start.2 = (bf16[192,2560]{1,0:T(8,128)(2,1)S(1)}, bf16[192,2560]{1,0:T(8,128)(2,1)S(1)}, u32[]{:S(2)}, u32[]{:S(2)}) collective-permute-start(bf16[192,2560]{1,0:T(8,128)(2,1)S(1)} %collective-permute-done), channel_id=1, source_target_pairs={{0,1},{1,4},{4,5},{5,8},{8,9},{9,12},{12,13},{13,0},{2,3},{3,6},{6... | collective-permute-start | bytes 2949128 | tf_op jit(solution)/shard_map/ppermute | solution.py:31
  47.8 1.0 copy-start.3
  48.7 45.8 %collective-permute-start.3 = (bf16[192,2560]{1,0:T(8,128)(2,1)S(1)}, bf16[192,2560]{1,0:T(8,128)(2,1)}, u32[]{:S(2)}, u32[]{:S(2)}) collective-permute-start(bf16[192,2560]{1,0:T(8,128)(2,1)S(1)} %collective-permute-done.1), channel_id=1, source_target_pairs={{0,13},{1,0},{4,1},{5,4},{8,5},{9,8},{12,9},{13,12},{2,15},{3,2},{... | collective-permute-start | bytes 2949128 | tf_op jit(solution)/shard_map/ppermute | solution.py:36
  81.8 12.7 %copy-start.5 = (bf16[192,2560]{1,0:T(8,128)(2,1)}, bf16[192,2560]{1,0:T(8,128)(2,1)S(1)}, u32[]{:S(2)}) copy-start(bf16[192,2560]{1,0:T(8,128)(2,1)S(1)} %collective-permute-done.2) | copy-start | bytes 2949124
  81.8 40.4 %collective-permute-start.4 = (bf16[192,2560]{1,0:T(8,128)(2,1)S(1)}, bf16[192,2560]{1,0:T(8,128)(2,1)}, u32[]{:S(2)}, u32[]{:S(2)}) collective-permute-start(bf16[192,2560]{1,0:T(8,128)(2,1)S(1)} %collective-permute-done.2), channel_id=1, source_target_pairs={{0,1},{1,4},{4,5},{5,8},{8,9},{9,12},{12,13},{13,0},{2,3},{3,6},{6... | collective-permute-start | bytes 2949128 | tf_op jit(solution)/shard_map/ppermute | solution.py:31
  94.5 132.7 %collective-permute-start.5 = (bf16[192,2560]{1,0:T(8,128)(2,1)}, bf16[192,2560]{1,0:T(8,128)(2,1)}, u32[]{:S(2)}, u32[]{:S(2)}) collective-permute-start(bf16[192,2560]{1,0:T(8,128)(2,1)} %collective-permute-done.3), channel_id=1, source_target_pairs={{0,13},{1,0},{4,1},{5,4},{8,5},{9,8},{12,9},{13,12},{2,15},{3,2},{... | collective-permute-start | bytes 2949128 | tf_op jit(solution)/shard_map/ppermute | solution.py:36
  122.2 120.6 %collective-permute-start.6 = (bf16[192,2560]{1,0:T(8,128)(2,1)}, bf16[192,2560]{1,0:T(8,128)(2,1)}, u32[]{:S(2)}, u32[]{:S(2)}) collective-permute-start(bf16[192,2560]{1,0:T(8,128)(2,1)} %collective-permute-done.4), channel_id=1, source_target_pairs={{0,1},{1,4},{4,5},{5,8},{8,9},{9,12},{12,13},{13,0},{2,3},{3,6},{6... | collective-permute-start | bytes 2949128 | tf_op jit(solution)/shard_map/ppermute | solution.py:31
  129.8 6.6 %copy-start.12 = (u32[32]{0:T(128)S(1)}, u32[32]{0:T(128)}, u32[]{:S(2)}) copy-start(u32[32]{0:T(128)} %constant.149) | copy-start | bytes 388
  141.3 28.0 %copy-start.4 = (bf16[192,2560]{1,0:T(8,128)(2,1)S(1)}, bf16[192,2560]{1,0:T(8,128)(2,1)}, u32[]{:S(2)}) copy-start(bf16[192,2560]{1,0:T(8,128)(2,1)} %copy-done.3) | copy-start | bytes 2949124
  256.8 59.2 %copy-start.8 = (bf16[2560,64]{0,1:T(8,128)(2,1)S(1)}, bf16[2560,64]{0,1:T(8,128)(2,1)}, u32[]{:S(2)}) copy-start(bf16[2560,64]{0,1:T(8,128)(2,1)} %param.18) | copy-start | bytes 983044
  256.8 59.2 %copy-start.9 = (f32[2560]{0:T(1024)S(1)}, f32[2560]{0:T(1024)}, u32[]{:S(2)}) copy-start(f32[2560]{0:T(1024)} %param.17) | copy-start | bytes 30724
  256.8 59.2 %copy-start.10 = (f32[2560]{0:T(1024)S(1)}, f32[2560]{0:T(1024)}, u32[]{:S(2)}) copy-start(f32[2560]{0:T(1024)} %param.16) | copy-start | bytes 30724
  271.0 2.3 copy-start.2
  296.1 2.3 copy-start.2
  308.6 17.4 %copy-start.7 = (f32[3,8,16,16]{3,2,1,0:T(8,128)S(1)}, f32[3,8,16,16]{3,2,1,0:T(8,128)}, u32[]{:S(2)}) copy-start(f32[3,8,16,16]{3,2,1,0:T(8,128)} %param.19) | copy-start | bytes 73732
  326.7 3.3 collective-permute-start.7
  328.7 5.6 %collective-permute-start.8 = (bf16[3,1,16,16]{3,2,1,0:T(8,128)(2,1)S(1)}, bf16[3,1,16,16]{3,2,1,0:T(8,128)(2,1)S(1)}, u32[]{:S(2)}, u32[]{:S(2)}) collective-permute-start(bf16[3,1,16,16]{3,2,1,0:T(8,128)(2,1)S(1)} %get-tuple-element.259), channel_id=1, source_target_pairs={{2,0},{3,1},{6,4},{7,5},{10,8},{11,9},{14,12},{15,13},{18,16},{19,... | collective-permute-start | bytes 4616 | tf_op jit(solution)/shard_map/ppermute | solution.py:57
  334.3 3.3 collective-permute-start.9
  335.6 3.1 collective-permute-start.10
  338.8 17.1 %collective-permute-start.11 = (bf16[2,10,18,16]{3,2,1,0:T(8,128)(2,1)S(1)}, bf16[2,10,18,16]{3,2,1,0:T(8,128)(2,1)S(1)}, u32[]{:S(2)}, u32[]{:S(2)}) collective-permute-start(bf16[2,10,18,16]{3,2,1,0:T(8,128)(2,1)S(1)} %pad_maximum_fusion.1), channel_id=1, source_target_pairs={{0,4},{4,8},{8,12},{1,5},{5,9},{9,13},{2,6},{6,10},{10,14},{3,7},{... | collective-permute-start | bytes 34568 | tf_op jit(solution)/shard_map/ppermute | solution.py:67
  353.0 7.1 %copy-start.11 = (f32[384]{0:T(512)S(1)}, f32[384]{0:T(512)}, u32[]{:S(2)}) copy-start(f32[384]{0:T(512)} %param.21) | copy-start | bytes 4612
  355.8 6.5 %copy-start.1 = (bf16[384,2560]{1,0:T(8,128)(2,1)S(1)}, bf16[384,2560]{1,0:T(8,128)(2,1)}, u32[]{:S(2)}) copy-start(bf16[384,2560]{1,0:T(8,128)(2,1)} %param.12) | copy-start | bytes 5898244
Sparse Core Ops, SparseCore 0:
  9.7 130.5 all-gather.1
